TPU v7x, 32 devices: a whole 2x2x4 slice. The times are simulated.
32 devices in a mesh: cand: 4 (over x, core), seq: 8 (over z, y).
Axes of the slice: x: 2, y: 2, z: 4, core: 2. Of those that a mesh axis runs over, the one named last changes fastest.
Arguments:
- latent: bfloat16 [4, 384, 3072], P('cand', 'seq'), may hold values from -0.59765625 to 0.59765625
- timesteps: int32 [4], replicated, may hold values from 0 to 999
- positions: int32 [3, 384], replicated, may hold values from 0 to 63
- mod_weight: bfloat16 [3072, 9216], P('cand', 'seq'), may hold values from -0.109375 to 0.109375
- input_weight: bfloat16 [3072, 16, 384], P('cand', 'seq'), may hold values from -0.109375 to 0.109375
- output_weight: bfloat16 [16, 128, 3072], P('seq', None, 'cand'), may hold values from -0.75 to 0.75
- cotangent: bfloat16 [4, 384, 3072], P('cand', 'seq'), may hold values from -6 to 6
Outputs:
- block_out: bfloat16 [4, 384, 3072], P('cand', 'seq')
- latent_grad: float32 [4, 384, 3072], P('cand', 'seq')
All inputs are finite; a program needn't handle non-finite values.
Results may differ from a plain program's by a relative error of at most 0.033.
Values may be sent and summed in bfloat16 or wider, within the bound.
A program may use at most 128 MiB of HBM per device.

v0:
```python
import jax
import jax.numpy as jnp
import numpy as np
from jax import lax
from jax.sharding import PartitionSpec as P

HEAD = 128
epsilon = 1e-06


def time_embed(timesteps, feature_width):
    half_size = feature_width // 2
    freq_rate = jnp.exp(-jnp.log(10000.0) * jnp.arange(half_size, dtype=jnp.float32) / half_size)
    angles = timesteps.astype(jnp.float32)[:, None] * freq_rate[None, :]
    return jnp.concatenate([jnp.cos(angles), jnp.sin(angles)], axis=1)


def rope_tables(positions, head_size):
    first_size = head_size // 8
    other_size = (head_size - first_size) // 2
    pieces = []
    swapped = []
    sign_vec = []
    offset = 0
    for axis_id, width_part in enumerate((first_size, other_size, other_size)):
        half_size = width_part // 2
        freq_rate = jnp.exp(
            -jnp.log(256.0) * 2.0 * jnp.arange(half_size, dtype=jnp.float32) / width_part
        )
        angle_part = positions[axis_id].astype(jnp.float32)[:, None] * freq_rate[None, :]
        pieces.append(angle_part)
        pieces.append(angle_part)
        swapped += list(range(offset + half_size, offset + width_part)) + list(
            range(offset, offset + half_size)
        )
        sign_vec += [-1.0] * half_size + [1.0] * half_size
        offset += width_part
    angles = jnp.concatenate(pieces, axis=1)
    return (
        jnp.cos(angles),
        jnp.sin(angles),
        np.array(swapped, np.int32),
        np.array(sign_vec, np.float32),
    )


def rotate(values, tables):
    cos_tab, sin_tab, swapped, sign_vec = tables
    return values * cos_tab + values[..., swapped] * sign_vec * sin_tab


def unrotate(values, tables):
    cos_tab, sin_tab, swapped, sign_vec = tables
    return values * cos_tab - (values * sin_tab)[..., swapped] * sign_vec


def rms_norm(values):
    inverse = lax.rsqrt(jnp.mean(values * values, -1, keepdims=True) + epsilon)
    return (values * inverse, inverse)


def rms_back(d_normed, normed, inverse):
    return inverse * (d_normed - normed * jnp.mean(d_normed * normed, -1, keepdims=True))


def layer_norm(values):
    centred = values - jnp.mean(values, -1, keepdims=True)
    inverse_std = lax.rsqrt(jnp.mean(centred * centred, -1, keepdims=True) + epsilon)
    return (centred * inverse_std, inverse_std)


def layer_norm_back(d_normed, normed, inverse_std):
    return inverse_std * (
        d_normed
        - jnp.mean(d_normed, -1, keepdims=True)
        - normed * jnp.mean(d_normed * normed, -1, keepdims=True)
    )


def times_transposed(left, right):
    return lax.dot_general(
        left, right, (((1,), (1,)), ((), ())), preferred_element_type=jnp.float32
    )


def attend(projected, tables):
    length, groups, triple = projected.shape
    head_size = triple // 3
    grouped = jnp.transpose(projected.reshape(length, groups, 3, head_size), (2, 1, 0, 3))
    query_n, query_inv = rms_norm(grouped[0])
    key_n, key_inv = rms_norm(grouped[1])
    q_rot = rotate(query_n, tables).astype(jnp.bfloat16)
    k_rot = rotate(key_n, tables).astype(jnp.bfloat16)
    values = grouped[2].astype(jnp.bfloat16)
    score_scale = head_size ** (-0.5)
    scores = (
        jnp.einsum("gld,gmd->glm", q_rot, k_rot, preferred_element_type=jnp.float32) * score_scale
    )
    weights = jnp.exp(scores - head_size**0.5)
    probs = weights / jnp.sum(weights, -1, keepdims=True)
    probs_low = probs.astype(jnp.bfloat16)
    heads_out = jnp.einsum("glm,gmd->gld", probs_low, values, preferred_element_type=jnp.float32)
    attended = (
        jnp.transpose(heads_out, (1, 0, 2)).reshape(length, groups * head_size).astype(jnp.bfloat16)
    )
    saved = (q_rot, k_rot, values, probs, probs_low, query_n, query_inv, key_n, key_inv)
    return (attended, saved)


def attend_back(d_attended, saved, tables):
    q_rot, k_rot, values, probs, probs_low, query_n, query_inv, key_n, key_inv = saved
    groups, length, head_size = q_rot.shape
    score_scale = head_size ** (-0.5)
    d_heads = jnp.transpose(d_attended.reshape(length, groups, head_size), (1, 0, 2))
    d_values = jnp.einsum("glm,gld->gmd", probs_low, d_heads, preferred_element_type=jnp.float32)
    d_probs = jnp.einsum("gld,gmd->glm", d_heads, values, preferred_element_type=jnp.float32)
    d_scores = (probs * (d_probs - jnp.sum(probs * d_probs, -1, keepdims=True))).astype(
        jnp.bfloat16
    )
    d_qrot = (
        jnp.einsum("glm,gmd->gld", d_scores, k_rot, preferred_element_type=jnp.float32)
        * score_scale
    )
    d_krot = (
        jnp.einsum("glm,gld->gmd", d_scores, q_rot, preferred_element_type=jnp.float32)
        * score_scale
    )
    d_query = rms_back(unrotate(d_qrot, tables), query_n, query_inv)
    d_key = rms_back(unrotate(d_krot, tables), key_n, key_inv)
    stacked = jnp.stack([d_query, d_key, d_values], 0)
    return (
        jnp.transpose(stacked, (2, 1, 0, 3))
        .reshape(length, groups * 3 * head_size)
        .astype(jnp.bfloat16)
    )


def on_device(latent, timesteps, positions, mod_weight, input_weight, output_weight, cotangent):
    width = latent.shape[2]
    rows_local = latent.shape[1]
    groups = input_weight.shape[1]
    group_cols = groups * input_weight.shape[2]
    time_act = jax.nn.silu(time_embed(timesteps, width)).astype(jnp.bfloat16)
    slab_rows = mod_weight.shape[0]
    act_rows = lax.dynamic_slice_in_dim(time_act, lax.axis_index("cand") * slab_rows, slab_rows, 1)
    mod_mine = lax.psum_scatter(
        jnp.dot(act_rows, mod_weight, preferred_element_type=jnp.float32).astype(jnp.bfloat16),
        "cand",
        scatter_dimension=0,
        tiled=True,
    ).astype(jnp.float32)
    modulation = lax.all_gather(mod_mine, "seq", axis=1, tiled=True)[0]
    shift_vec = modulation[:width]
    scale_vec = modulation[width : 2 * width]
    gate_vec = modulation[2 * width :]
    latent_rows = latent[0].astype(jnp.float32)
    normed, inverse_std = layer_norm(latent_rows)
    modulated = (normed * (1.0 + scale_vec) + shift_vec).astype(jnp.bfloat16)
    gathered = lax.all_gather(modulated, "seq", axis=0, tiled=True)
    length = gathered.shape[0]
    tables = rope_tables(positions, HEAD)
    piece = lax.all_gather(input_weight, "cand", axis=0, tiled=True)
    projected = jnp.dot(
        gathered, piece.reshape(piece.shape[0], group_cols), preferred_element_type=jnp.float32
    )
    attended, saved = attend(projected.reshape(length, groups, 3 * HEAD), tables)
    w_heads = lax.all_gather(output_weight, "seq", axis=0, tiled=True)
    w_all = lax.all_gather(w_heads, "cand", axis=2, tiled=True)
    w_all = w_all.reshape(w_all.shape[0] * w_all.shape[1], width)
    token_heads = lax.all_to_all(attended, "seq", split_axis=0, concat_axis=1, tiled=True)
    mixed = jnp.dot(token_heads, w_all, preferred_element_type=jnp.float32)
    block_out = (latent_rows + gate_vec * mixed).astype(jnp.bfloat16)
    d_mixed = (cotangent[0].astype(jnp.float32) * gate_vec).astype(jnp.bfloat16)
    d_tokens = times_transposed(d_mixed, w_all).astype(jnp.bfloat16)
    d_attended = lax.all_to_all(d_tokens, "seq", split_axis=1, concat_axis=0, tiled=True)
    d_projected = attend_back(d_attended, saved, tables)
    w_back = lax.all_gather(input_weight, "cand", axis=0, tiled=True).reshape(width, group_cols)
    d_modulated = lax.psum_scatter(
        times_transposed(
            lax.slice_in_dim(d_projected, 0, rows_local * lax.axis_size("seq"), axis=0), w_back
        ).astype(jnp.bfloat16),
        "seq",
        scatter_dimension=0,
        tiled=True,
    ).astype(jnp.float32)
    latent_grad = cotangent[0].astype(jnp.float32) + layer_norm_back(
        d_modulated * (1.0 + scale_vec), normed, inverse_std
    )
    return (block_out[None], latent_grad[None])


def solution(mesh):
    placed = (
        P("cand", "seq", None),
        P(),
        P(),
        P("cand", "seq"),
        P("cand", "seq", None),
        P("seq", None, "cand"),
        P("cand", "seq", None),
    )
    return jax.shard_map(
        on_device,
        mesh=mesh,
        in_specs=placed,
        out_specs=(P("cand", "seq", None), P("cand", "seq", None)),
        check_vma=False,
    )
```

profile of v0, /device:TPU:0, one launch (start us, length us, event | category | flops | bytes accessed | tf_op | source)
XLA Modules:
  0.0 380.3 jit_solution(16041550091423698796)
XLA Ops:
  7.2 0.7 all-gather.9.cloned.1.call-update
  8.0 0.7 all-gather.7.cloned.1.call-update
  8.8 0.6 dynamic-slice
  9.4 0.3 multiply_cosine_fusion
  9.7 0.3 convolution_convert_fusion.2
  10.0 8.7 %all-reduce = bf16[4,1152]{1,0:T(4,128)(2,1)S(1)} all-reduce(bf16[4,1152]{1,0:T(4,128)(2,1)S(1)} %convolution_convert_fusion.2), channel_id=2, replica_groups=mesh['cand'=4,'seq'=8] {'cand'}, use_global_device_ids=true, to_apply=%region_0.1.clone | all-reduce | flops 4608 | bytes 18432
  18.7 0.7 dynamic-slice_convert_fusion
  19.4 31.6 %all_gather.16 = f32[1,9216]{1,0:T(1,128)S(1)} all-gather(f32[1,1152]{1,0:T(1,128)S(1)} %dynamic-slice_convert_fusion), channel_id=1, replica_groups=mesh['cand'=4,'seq'=8] {'seq'}, dimensions={1}, use_global_device_ids=true | all-gather | bytes 41472 | tf_op jit(solution)/shard_map/all_gather | solution.py:152
  51.0 0.2 convert_reduce_fusion
  51.1 0.3 fusion.25
  51.4 0.9 fusion.19
  52.4 20.8 %all-gather.9.cloned.1.call-done = bf16[16,128,768]{2,1,0:T(8,128)(2,1)} async-done(((bf16[2,128,768]{2,1,0:T(8,128)(2,1)}), bf16[16,128,768]{2,1,0:T(8,128)(2,1)}) %all-gather.9.cloned.1.call-update) | async-done | bytes 3145744 | tf_op jit(solution)/shard_map/all_gather | solution.py:167
  73.2 0.6 copy-done.25
  73.9 0.1 broadcast_multiply_fusion.6
  74.0 0.1 broadcast_multiply_fusion.4
  74.0 0.3 concatenate.15
  74.4 0.6 pad_clamp_fusion
  74.9 0.7 fusion.61
  75.6 0.8 broadcast_multiply_fusion.2
  76.4 34.5 %all-gather.7.cloned.1.call-done = bf16[3072,2,384]{2,1,0:T(2,128)(2,1)} async-done(((bf16[768,2,384]{2,1,0:T(2,128)(2,1)}), bf16[3072,2,384]{2,1,0:T(2,128)(2,1)}) %all-gather.7.cloned.1.call-update) | async-done | bytes 4718608 | tf_op jit(solution)/shard_map/all_gather | solution.py:162
  110.9 5.2 %copy.89 = bf16[384,8,2,384]{3,1,2,0:T(8,128)(2,1)} copy(bf16[384,8,2,384]{3,2,1,0:T(2,128)(2,1)} %bitcast.149) | data formatting | bytes 9437184
  116.1 6.7 %copy.50 = bf16[3072,768]{0,1:T(8,128)(2,1)} copy(bf16[3072,768]{1,0:T(8,128)(2,1)} %bitcast.145) | data formatting | bytes 9437184 | tf_op jit(solution)/shard_map/reshape | solution.py:164
  122.8 42.7 %all-gather.5.cloned.1.call-done = bf16[384,3072]{1,0:T(8,128)(2,1)} async-done(((bf16[48,3072]{1,0:T(8,128)(2,1)}), bf16[384,3072]{1,0:T(8,128)(2,1)}) %all-gather.5.cloned.1.call-update) | async-done | bytes 2359312 | tf_op jit(solution)/shard_map/all_gather | solution.py:159
  165.5 5.3 %fusion.5 = f32[3,2,384,128]{2,3,0,1:T(8,128)S(1)} fusion(bf16[2,3,128,3072]{3,2,1,0:T(8,128)(2,1)} %bitcast.150, bf16[384,3072]{1,0:T(8,128)(2,1)} %all-gather.5.cloned.1.call-done), kind=kOutput, calls=%fused_computation.13 | convolution fusion | flops 1811939328 | bytes 8257536 | tf_op jit(solution)/shard_map/dot_general | solution.py:163
  170.8 1.0 copy-done.6
  171.8 0.1 multiply_reduce_fusion.3
  171.9 75.6 %all-gather.11.cloned.1.call-done = bf16[16,128,3072]{2,1,0:T(8,128)(2,1)} async-done(((bf16[16,128,768]{2,1,0:T(8,128)(2,1)}), bf16[16,128,3072]{2,1,0:T(8,128)(2,1)}) %all-gather.11.cloned.1.call-update) | async-done | bytes 12582928 | tf_op jit(solution)/shard_map/all_gather | solution.py:168
  247.6 8.5 %convolution_convert_fusion.1 = bf16[48,2048]{1,0:T(8,128)(2,1)S(1)} fusion(bf16[2048,3072]{1,0:T(8,128)(2,1)} %bitcast.143, bf16[1,48,3072]{2,1,0:T(8,128)(2,1)S(1)} %copy-done.10, f32[3072]{0:T(1024)S(1)} %bitcast.159), kind=kOutput, calls=%fused_computation.11 | convolution fusion | flops 604520448 | bytes 13086720 | tf_op jit(solution)/shard_map/dot_general | solution.py:81
  256.0 0.7 copy.119
  256.7 5.5 %all-to-all-start.1 = ((bf16[48,8,256]{2,0,1:T(8,128)(2,1)}), bf16[48,8,256]{2,0,1:T(8,128)(2,1)S(1)}, u32[]{:S(2)}, u32[]{:S(2)}) async-start(bf16[48,8,256]{2,0,1:T(8,128)(2,1)} %bitcast.142), calls=%async_computation.1 | async-start | bytes 393216 | tf_op jit(solution)/shard_map/all_to_all | solution.py:175
  262.2 0.2 reduce-scatter.2.cloned.1.call-start
  262.5 1.2 fusion.35
  263.7 1.1 copy.52
  264.8 1.0 copy.54
  265.8 2.2 gather_fusion
  268.0 2.9 gather_fusion.1
  270.9 1.9 fusion.31
  272.9 2.5 fusion.45
  275.3 2.1 multiply_reduce_fusion
  277.5 1.1 fusion.11
  278.5 0.2 copy-done.7
  278.7 0.2 multiply_convert_fusion
  278.9 0.8 copy-done.14
  279.7 0.3 fusion.63
  280.0 0.6 copy-done.13
  280.6 0.1 copy-done.15
  280.7 1.1 broadcast_multiply_fusion
  281.8 1.0 copy.69
  282.8 2.9 gather_fusion.3
  285.7 2.0 copy.66
  287.8 2.9 gather_fusion.2
  290.6 2.0 multiply_reduce_fusion.2
  292.7 2.0 fusion.41
  294.7 0.1 maximum_bitcast_fusion
  294.8 0.1 copy.73
  294.9 3.5 convolution_convert_fusion
  298.4 1.4 fusion.10
  299.8 0.2 copy.60
  300.0 0.1 convert_element_type.131
  300.2 18.7 %all_to_all.32 = bf16[8,48,256]{2,1,0:T(8,128)(2,1)S(1)} all-to-all(bf16[8,48,256]{2,1,0:T(8,128)(2,1)S(1)} %convert_element_type.131), channel_id=1, replica_groups=mesh['cand'=4,'seq'=8] {'seq'}, dimensions={0} | all-to-all | bytes 393216 | tf_op jit(solution)/shard_map/all_to_all | solution.py:170
  319.0 7.9 %fusion.2 = bf16[1,48,3072]{2,1,0:T(8,128)(2,1)} fusion(bf16[48,2048]{1,0:T(8,128)(2,1)S(1)} %bitcast.151, bf16[2048,3072]{1,0:T(8,128)(2,1)} %bitcast.144, bf16[1,48,3072]{2,1,0:T(8,128)(2,1)S(1)} %copy-done.2, f32[3072]{0:T(1024)S(1)} %bitcast.160), kind=kOutput, calls=%fused_computation.8 | convolution fusion | flops 604569600 | bytes 13381632 | tf_op jit(solution)/shard_map/dot_general | solution.py:171
  326.9 43.6 %reduce-scatter.2.cloned.1.call-done = bf16[48,3072]{1,0:T(8,128)(2,1)} async-done(((bf16[384,3072]{1,0:T(8,128)(2,1)}), bf16[48,3072]{1,0:T(8,128)(2,1)}) %reduce-scatter.2.cloned.1.call-update) | async-done | bytes 294928 | tf_op jit(solution)/shard_map/reduce_scatter | solution.py:178
  370.5 1.2 fusion.27
  371.8 2.0 fusion.24
  (80 shorter events, 0.5 us)
Async XLA Ops:
  7.2 2.5 copy-start
  7.2 1.6 copy-start.28
  7.2 1.6 copy-start.27
  7.2 66.0 %all-gather.9.cloned.1.call-start = ((), (), s32[]{:S(2)}) async-start(), calls=%async_computation.5 | async-start | bytes 3538944 | tf_op jit(solution)/shard_map/all_gather | solution.py:167
  7.9 103.0 %all-gather.7.cloned.1.call-start = ((), (), s32[]{:S(2)}) async-start(), calls=%async_computation.4 | async-start | bytes 5898240 | tf_op jit(solution)/shard_map/all_gather | solution.py:162
  8.7 42.3 %copy-start.1 = (bf16[1,48,3072]{2,1,0:T(8,128)(2,1)S(1)}, bf16[1,48,3072]{2,1,0:T(8,128)(2,1)}, u32[]{:S(2)}) copy-start(bf16[1,48,3072]{2,1,0:T(8,128)(2,1)} %param.13) | copy-start | bytes 884740
  8.7 156.8 %all-gather.5.cloned.1.call-start = ((), (), s32[]{:S(2)}) async-start(), calls=%async_computation.3 | async-start | bytes 2654208 | tf_op jit(solution)/shard_map/all_gather | solution.py:159
  51.1 22.1 %copy-start.20 = (f32[48]{0:T(128)}, f32[48]{0:T(128)S(1)}, u32[]{:S(2)}) copy-start(f32[48]{0:T(128)S(1)} %broadcast_multiply_fusion.11) | copy-start | bytes 580
  51.4 21.8 %copy-start.23 = (f32[48]{0:T(128)}, f32[48]{0:T(128)S(1)}, u32[]{:S(2)}) copy-start(f32[48]{0:T(128)S(1)} %add_rsqrt_fusion.2) | copy-start | bytes 580
  51.4 196.1 %copy-start.16 = (f32[1,3072]{1,0:T(1,128)}, f32[1,3072]{1,0:T(1,128)S(1)}, u32[]{:S(2)}) copy-start(f32[1,3072]{1,0:T(1,128)S(1)} %get-tuple-element.21) | copy-start | bytes 36868
  52.4 195.2 %all-gather.11.cloned.1.call-start = ((), (), s32[]{:S(2)}) async-start(), calls=%async_computation.6 | async-start | bytes 15728640 | tf_op jit(solution)/shard_map/all_gather | solution.py:168
  73.2 0.7 copy-start.25
  73.2 1.2 copy-start.26
  165.5 82.1 %copy-start.10 = (bf16[1,48,3072]{2,1,0:T(8,128)(2,1)S(1)}, bf16[1,48,3072]{2,1,0:T(8,128)(2,1)}, u32[]{:S(2)}) copy-start(bf16[1,48,3072]{2,1,0:T(8,128)(2,1)} %param.19) | copy-start | bytes 884740
  170.8 1.1 copy-start.6
  171.9 90.5 %copy-start.18 = (f32[2,384]{1,0:T(2,128)}, f32[2,384]{1,0:T(2,128)S(1)}, u32[]{:S(2)}) copy-start(f32[2,384]{1,0:T(2,128)S(1)} %get-tuple-element.32) | copy-start | bytes 9220
  256.7 16.1 %all-to-all-start.1 = ((bf16[48,8,256]{2,0,1:T(8,128)(2,1)}), bf16[48,8,256]{2,0,1:T(8,128)(2,1)S(1)}, u32[]{:S(2)}, u32[]{:S(2)}) async-start(bf16[48,8,256]{2,0,1:T(8,128)(2,1)} %bitcast.142), calls=%async_computation.1 | async-start | bytes 393216 | tf_op jit(solution)/shard_map/all_to_all | solution.py:175
  262.2 108.2 %reduce-scatter.2.cloned.1.call-start = ((), (), s32[]{:S(2)}) async-start(), calls=%async_computation.7 | async-start | bytes 2654208 | tf_op jit(solution)/shard_map/reduce_scatter | solution.py:178
  263.7 11.7 %copy-start.3 = (f32[2,384,128]{1,2,0:T(8,128)}, f32[2,384,128]{1,2,0:T(8,128)S(1)}, u32[]{:S(2)}) copy-start(f32[2,384,128]{1,2,0:T(8,128)S(1)} %get-tuple-element.11) | copy-start | bytes 1179652
  263.7 11.7 %copy-start.4 = (f32[2,384,128]{1,2,0:T(8,128)}, f32[2,384,128]{1,2,0:T(8,128)S(1)}, u32[]{:S(2)}) copy-start(f32[2,384,128]{1,2,0:T(8,128)S(1)} %get-tuple-element.12) | copy-start | bytes 1179652
  272.8 2.5 copy-start.8
  275.3 2.1 copy-start.9
  277.5 1.3 copy-start.7
  278.7 0.9 copy-start.14
  279.7 0.9 copy-start.13
  279.7 1.0 copy-start.15
  279.9 1.9 copy-start.5
  281.8 13.1 %slice-start = ((s8[4718592]{0:T(1024)(128)(4,1)}), s8[524288]{0:T(1024)(128)(4,1)S(1)}, s32[]{:S(2)}) async-start(s8[4718592]{0:T(1024)(128)(4,1)} %bitcast.146), calls=%async_computation.8 | async-start | bytes 1048576
  282.8 7.8 %copy-start.22 = (f32[128]{0:T(128)S(1)}, f32[128]{0:T(128)}, u32[]{:S(2)}) copy-start(f32[128]{0:T(128)} %constant.63.clone) | copy-start | bytes 1540
  287.8 4.9 %copy-start.19 = (f32[2,384]{1,0:T(2,128)S(1)}, f32[2,384]{1,0:T(2,128)}, u32[]{:S(2)}) copy-start(f32[2,384]{1,0:T(2,128)} %copy-done.18) | copy-start | bytes 9220
  290.6 4.2 %slice-start.1 = ((s8[4718592]{0:T(1024)(128)(4,1)}), s8[4194304]{0:T(1024)(128)(4,1)S(1)}, s32[]{:S(2)}) async-start(s8[4718592]{0:T(1024)(128)(4,1)} %bitcast.146), calls=%async_computation.9 | async-start | bytes 8388608
  292.7 2.0 copy-start.12
  299.8 19.1 %copy-start.2 = (bf16[1,48,3072]{2,1,0:T(8,128)(2,1)S(1)}, bf16[1,48,3072]{2,1,0:T(8,128)(2,1)}, u32[]{:S(2)}) copy-start(bf16[1,48,3072]{2,1,0:T(8,128)(2,1)} %param.13) | copy-start | bytes 884740
  299.8 19.1 %copy-start.17 = (f32[1,3072]{1,0:T(1,128)S(1)}, f32[1,3072]{1,0:T(1,128)}, u32[]{:S(2)}) copy-start(f32[1,3072]{1,0:T(1,128)} %copy-done.16) | copy-start | bytes 36868
  318.9 51.6 %copy-start.21 = (f32[48]{0:T(128)S(1)}, f32[48]{0:T(128)}, u32[]{:S(2)}) copy-start(f32[48]{0:T(128)} %copy-done.20) | copy-start | bytes 580
  318.9 51.6 %copy-start.24 = (f32[48]{0:T(128)S(1)}, f32[48]{0:T(128)}, u32[]{:S(2)}) copy-start(f32[48]{0:T(128)} %copy-done.23) | copy-start | bytes 580
  318.9 52.8 %copy-start.11 = (bf16[1,48,3072]{2,1,0:T(8,128)(2,1)S(1)}, bf16[1,48,3072]{2,1,0:T(8,128)(2,1)}, u32[]{:S(2)}) copy-start(bf16[1,48,3072]{2,1,0:T(8,128)(2,1)} %param.19) | copy-start | bytes 884740
Sparse Core Ops, SparseCore 0:
  10.2 62.9 all-gather.8
  74.7 36.1 all-gather.6
  113.7 51.8 all-gather.4
  166.9 80.6 all-gather.10
  298.5 71.9 reduce-scatter.1
where the time goes:
time: 381 us; the launch traced here: 380 us
  waiting for transfers between devices  219 us (57%)
  blocking collectives  59 us (15%)
  local copies, waits for them, and re-layouts  34.1 us (9%)
  matrix products  33.8 us (9%)
  other arithmetic  14.5 us (4%)
  between operations  14.3 us (4%)
  starting transfers between devices  5.89 us (2%)
    all_gather x1, waiting for transfers between devices, on_device(): w_all = lax.all_gather(w_heads, 'cand', axis=2, tiled=True)  75.6 us
    reduce_scatter x1, waiting for transfers between devices, on_device(): lax.psum_scatter(times_transposed(lax.slice_in_dim(d_projected, 0, rows_l...  43.6 us
    all_gather x1, waiting for transfers between devices, on_device(): gathered = lax.all_gather(modulated, 'seq', axis=0, tiled=True)  42.7 us
    all_gather x1, waiting for transfers between devices, on_device(): piece = lax.all_gather(input_weight, 'cand', axis=0, tiled=True)  34.5 us
    all_gather x1, blocking collectives, on_device(): modulation = lax.all_gather(mod_mine, 'seq', axis=1, tiled=True)[0]  31.6 us
    all_gather x1, waiting for transfers between devices, on_device(): w_heads = lax.all_gather(output_weight, 'seq', axis=0, tiled=True)  20.8 us
    all_to_all x1, blocking collectives, on_device(): lax.all_to_all(attended, 'seq', split_axis=0, concat_axis=1, tiled=True)  18.7 us
    dot_general x2, matrix products, times_transposed(): lax.dot_general(left, right, (((1,), (1,)), ((), ())), preferred_element_...  11.9 us
  transfers between devices with their start and end apart: 6, of which 5 were waited for; matrix products, arithmetic and copies ran while one was open for 11% of the time, Pallas kernels for 0%

commit v1 on v0

--- a/solution.py
+++ b/solution.py
@@ -149,7 +149,7 @@
         scatter_dimension=0,
         tiled=True,
     ).astype(jnp.float32)
-    modulation = lax.all_gather(mod_mine, "seq", axis=1, tiled=True)[0]
+    modulation = jnp.concatenate(lax.all_gather(mod_mine, "seq"), axis=1)[0]
     shift_vec = modulation[:width]
     scale_vec = modulation[width : 2 * width]
     gate_vec = modulation[2 * width :]

time: 381 us -> 381 us (level)
  no operation moved by 1% of the time
where the time goes in v1:
time: 381 us; the launch traced here: 380 us
  waiting for transfers between devices  219 us (57%)
  blocking collectives  59 us (15%)
  local copies, waits for them, and re-layouts  34.1 us (9%)
  matrix products  33.8 us (9%)
  other arithmetic  14.5 us (4%)
  between operations  14.3 us (4%)
  starting transfers between devices  5.89 us (2%)
    all_gather x1, waiting for transfers between devices, on_device(): w_all = lax.all_gather(w_heads, 'cand', axis=2, tiled=True)  75.6 us
    reduce_scatter x1, waiting for transfers between devices, on_device(): lax.psum_scatter(times_transposed(lax.slice_in_dim(d_projected, 0, rows_l...  43.6 us
    all_gather x1, waiting for transfers between devices, on_device(): gathered = lax.all_gather(modulated, 'seq', axis=0, tiled=True)  42.7 us
    all_gather x1, waiting for transfers between devices, on_device(): piece = lax.all_gather(input_weight, 'cand', axis=0, tiled=True)  34.5 us
    all_gather x1, blocking collectives, on_device(): modulation = jnp.concatenate(lax.all_gather(mod_mine, 'seq'), axis=1)[0]  31.6 us
    all_gather x1, waiting for transfers between devices, on_device(): w_heads = lax.all_gather(output_weight, 'seq', axis=0, tiled=True)  20.8 us
    all_to_all x1, blocking collectives, on_device(): lax.all_to_all(attended, 'seq', split_axis=0, concat_axis=1, tiled=True)  18.7 us
    dot_general x2, matrix products, times_transposed(): lax.dot_general(left, right, (((1,), (1,)), ((), ())), preferred_element_...  11.9 us
  transfers between devices with their start and end apart: 6, of which 5 were waited for; matrix products, arithmetic and copies ran while one was open for 11% of the time, Pallas kernels for 0%

profile of v1, /device:TPU:0, one launch (start us, length us, event | category | flops | bytes accessed | tf_op | source)
XLA Modules:
  0.0 380.3 jit_solution(220136956483584241)
XLA Ops:
  7.2 0.7 all-gather.11.cloned.1.call-update
  8.0 0.7 all-gather.9.cloned.1.call-update
  8.8 0.6 dynamic-slice
  9.4 0.3 multiply_cosine_fusion
  9.7 0.3 convolution_convert_fusion.2
  10.0 8.7 %all-reduce = bf16[4,1152]{1,0:T(4,128)(2,1)S(1)} all-reduce(bf16[4,1152]{1,0:T(4,128)(2,1)S(1)} %convolution_convert_fusion.2), channel_id=3, replica_groups=mesh['cand'=4,'seq'=8] {'cand'}, use_global_device_ids=true, to_apply=%region_0.1.clone | all-reduce | flops 4608 | bytes 18432
  18.7 0.7 bitcast_convert_fusion
  19.4 31.6 %all-gather.1 = f32[8,1,1152]{2,1,0:T(1,128)S(1)} all-gather(f32[1,1,1152]{2,1,0:T(1,128)S(1)} %bitcast_convert_fusion), channel_id=2, replica_groups=mesh['cand'=4,'seq'=8] {'seq'}, dimensions={0}, use_global_device_ids=true | all-gather | bytes 41472 | tf_op jit(solution)/shard_map/all_gather | solution.py:152
  51.0 0.2 convert_reduce_fusion
  51.1 0.3 fusion.25
  51.4 0.9 fusion.19
  52.4 20.8 %all-gather.11.cloned.1.call-done = bf16[16,128,768]{2,1,0:T(8,128)(2,1)} async-done(((bf16[2,128,768]{2,1,0:T(8,128)(2,1)}), bf16[16,128,768]{2,1,0:T(8,128)(2,1)}) %all-gather.11.cloned.1.call-update) | async-done | bytes 3145744 | tf_op jit(solution)/shard_map/all_gather | solution.py:167
  73.2 0.6 copy-done.25
  73.9 0.1 broadcast_multiply_fusion.6
  74.0 0.1 broadcast_multiply_fusion.4
  74.0 0.3 concatenate.15
  74.4 0.6 pad_clamp_fusion
  74.9 0.7 fusion.61
  75.6 0.8 broadcast_multiply_fusion.2
  76.4 34.5 %all-gather.9.cloned.1.call-done = bf16[3072,2,384]{2,1,0:T(2,128)(2,1)} async-done(((bf16[768,2,384]{2,1,0:T(2,128)(2,1)}), bf16[3072,2,384]{2,1,0:T(2,128)(2,1)}) %all-gather.9.cloned.1.call-update) | async-done | bytes 4718608 | tf_op jit(solution)/shard_map/all_gather | solution.py:162
  110.9 5.2 %copy.89 = bf16[384,8,2,384]{3,1,2,0:T(8,128)(2,1)} copy(bf16[384,8,2,384]{3,2,1,0:T(2,128)(2,1)} %bitcast.150) | data formatting | bytes 9437184
  116.1 6.7 %copy.50 = bf16[3072,768]{0,1:T(8,128)(2,1)} copy(bf16[3072,768]{1,0:T(8,128)(2,1)} %bitcast.146) | data formatting | bytes 9437184 | tf_op jit(solution)/shard_map/reshape | solution.py:164
  122.8 42.7 %all-gather.7.cloned.1.call-done = bf16[384,3072]{1,0:T(8,128)(2,1)} async-done(((bf16[48,3072]{1,0:T(8,128)(2,1)}), bf16[384,3072]{1,0:T(8,128)(2,1)}) %all-gather.7.cloned.1.call-update) | async-done | bytes 2359312 | tf_op jit(solution)/shard_map/all_gather | solution.py:159
  165.5 5.3 %fusion.5 = f32[3,2,384,128]{2,3,0,1:T(8,128)S(1)} fusion(bf16[2,3,128,3072]{3,2,1,0:T(8,128)(2,1)} %bitcast.151, bf16[384,3072]{1,0:T(8,128)(2,1)} %all-gather.7.cloned.1.call-done), kind=kOutput, calls=%fused_computation.13 | convolution fusion | flops 1811939328 | bytes 8257536 | tf_op jit(solution)/shard_map/dot_general | solution.py:163
  170.8 1.0 copy-done.6
  171.8 0.1 multiply_reduce_fusion.3
  171.9 75.6 %all-gather.13.cloned.1.call-done = bf16[16,128,3072]{2,1,0:T(8,128)(2,1)} async-done(((bf16[16,128,768]{2,1,0:T(8,128)(2,1)}), bf16[16,128,3072]{2,1,0:T(8,128)(2,1)}) %all-gather.13.cloned.1.call-update) | async-done | bytes 12582928 | tf_op jit(solution)/shard_map/all_gather | solution.py:168
  247.6 8.5 %convolution_convert_fusion.1 = bf16[48,2048]{1,0:T(8,128)(2,1)S(1)} fusion(bf16[2048,3072]{1,0:T(8,128)(2,1)} %bitcast.144, bf16[1,48,3072]{2,1,0:T(8,128)(2,1)S(1)} %copy-done.10, f32[3072]{0:T(1024)S(1)} %get-tuple-element.21), kind=kOutput, calls=%fused_computation.11 | convolution fusion | flops 604520448 | bytes 13086720 | tf_op jit(solution)/shard_map/dot_general | solution.py:81
  256.0 0.7 copy.119
  256.7 5.5 %all-to-all-start.1 = ((bf16[48,8,256]{2,0,1:T(8,128)(2,1)}), bf16[48,8,256]{2,0,1:T(8,128)(2,1)S(1)}, u32[]{:S(2)}, u32[]{:S(2)}) async-start(bf16[48,8,256]{2,0,1:T(8,128)(2,1)} %bitcast.143), calls=%async_computation.1 | async-start | bytes 393216 | tf_op jit(solution)/shard_map/all_to_all | solution.py:175
  262.2 0.2 reduce-scatter.2.cloned.1.call-start
  262.5 1.2 fusion.35
  263.7 1.1 copy.52
  264.8 1.0 copy.54
  265.8 2.2 gather_fusion
  268.0 2.9 gather_fusion.1
  270.9 1.9 fusion.31
  272.9 2.5 fusion.45
  275.3 2.1 multiply_reduce_fusion
  277.5 1.1 fusion.11
  278.5 0.2 copy-done.7
  278.7 0.2 multiply_convert_fusion
  278.9 0.8 copy-done.14
  279.7 0.3 fusion.63
  280.0 0.6 copy-done.13
  280.6 0.1 copy-done.15
  280.7 1.1 broadcast_multiply_fusion
  281.8 1.0 copy.69
  282.8 2.9 gather_fusion.3
  285.7 2.0 copy.66
  287.8 2.9 gather_fusion.2
  290.6 2.0 multiply_reduce_fusion.2
  292.7 2.0 fusion.41
  294.7 0.1 maximum_bitcast_fusion
  294.8 0.1 copy.73
  294.9 3.5 convolution_convert_fusion
  298.4 1.4 fusion.10
  299.8 0.2 copy.60
  300.0 0.1 convert_element_type.128
  300.2 18.7 %all_to_all.32 = bf16[8,48,256]{2,1,0:T(8,128)(2,1)S(1)} all-to-all(bf16[8,48,256]{2,1,0:T(8,128)(2,1)S(1)} %convert_element_type.128), channel_id=1, replica_groups=mesh['cand'=4,'seq'=8] {'seq'}, dimensions={0} | all-to-all | bytes 393216 | tf_op jit(solution)/shard_map/all_to_all | solution.py:170
  319.0 7.9 %fusion.2 = bf16[1,48,3072]{2,1,0:T(8,128)(2,1)} fusion(bf16[48,2048]{1,0:T(8,128)(2,1)S(1)} %bitcast.152, bf16[2048,3072]{1,0:T(8,128)(2,1)} %bitcast.145, bf16[1,48,3072]{2,1,0:T(8,128)(2,1)S(1)} %copy-done.2, f32[3072]{0:T(1024)S(1)} %copy-done.17), kind=kOutput, calls=%fused_computation.8 | convolution fusion | flops 604569600 | bytes 13381632 | tf_op jit(solution)/shard_map/dot_general | solution.py:171
  326.9 43.6 %reduce-scatter.2.cloned.1.call-done = bf16[48,3072]{1,0:T(8,128)(2,1)} async-done(((bf16[384,3072]{1,0:T(8,128)(2,1)}), bf16[48,3072]{1,0:T(8,128)(2,1)}) %reduce-scatter.2.cloned.1.call-update) | async-done | bytes 294928 | tf_op jit(solution)/shard_map/reduce_scatter | solution.py:178
  370.5 1.2 fusion.27
  371.8 2.0 fusion.24
  (80 shorter events, 0.5 us)
Async XLA Ops:
  7.2 2.5 copy-start
  7.2 1.6 copy-start.28
  7.2 1.6 copy-start.27
  7.2 66.0 %all-gather.11.cloned.1.call-start = ((), (), s32[]{:S(2)}) async-start(), calls=%async_computation.5 | async-start | bytes 3538944 | tf_op jit(solution)/shard_map/all_gather | solution.py:167
  7.9 103.0 %all-gather.9.cloned.1.call-start = ((), (), s32[]{:S(2)}) async-start(), calls=%async_computation.4 | async-start | bytes 5898240 | tf_op jit(solution)/shard_map/all_gather | solution.py:162
  8.7 42.3 %copy-start.1 = (bf16[1,48,3072]{2,1,0:T(8,128)(2,1)S(1)}, bf16[1,48,3072]{2,1,0:T(8,128)(2,1)}, u32[]{:S(2)}) copy-start(bf16[1,48,3072]{2,1,0:T(8,128)(2,1)} %param.13) | copy-start | bytes 884740
  8.7 156.8 %all-gather.7.cloned.1.call-start = ((), (), s32[]{:S(2)}) async-start(), calls=%async_computation.3 | async-start | bytes 2654208 | tf_op jit(solution)/shard_map/all_gather | solution.py:159
  51.1 22.1 %copy-start.20 = (f32[48]{0:T(128)}, f32[48]{0:T(128)S(1)}, u32[]{:S(2)}) copy-start(f32[48]{0:T(128)S(1)} %broadcast_multiply_fusion.11) | copy-start | bytes 580
  51.4 21.8 %copy-start.23 = (f32[48]{0:T(128)}, f32[48]{0:T(128)S(1)}, u32[]{:S(2)}) copy-start(f32[48]{0:T(128)S(1)} %add_rsqrt_fusion.2) | copy-start | bytes 580
  51.4 196.1 %copy-start.16 = (f32[3072]{0:T(1024)}, f32[3072]{0:T(1024)S(1)}, u32[]{:S(2)}) copy-start(f32[3072]{0:T(1024)S(1)} %get-tuple-element.21) | copy-start | bytes 36868
  52.4 195.2 %all-gather.13.cloned.1.call-start = ((), (), s32[]{:S(2)}) async-start(), calls=%async_computation.6 | async-start | bytes 15728640 | tf_op jit(solution)/shard_map/all_gather | solution.py:168
  73.2 0.7 copy-start.25
  73.2 1.2 copy-start.26
  165.5 82.1 %copy-start.10 = (bf16[1,48,3072]{2,1,0:T(8,128)(2,1)S(1)}, bf16[1,48,3072]{2,1,0:T(8,128)(2,1)}, u32[]{:S(2)}) copy-start(bf16[1,48,3072]{2,1,0:T(8,128)(2,1)} %param.19) | copy-start | bytes 884740
  170.8 1.1 copy-start.6
  171.9 90.5 %copy-start.18 = (f32[2,384]{1,0:T(2,128)}, f32[2,384]{1,0:T(2,128)S(1)}, u32[]{:S(2)}) copy-start(f32[2,384]{1,0:T(2,128)S(1)} %get-tuple-element.32) | copy-start | bytes 9220
  256.7 16.1 %all-to-all-start.1 = ((bf16[48,8,256]{2,0,1:T(8,128)(2,1)}), bf16[48,8,256]{2,0,1:T(8,128)(2,1)S(1)}, u32[]{:S(2)}, u32[]{:S(2)}) async-start(bf16[48,8,256]{2,0,1:T(8,128)(2,1)} %bitcast.143), calls=%async_computation.1 | async-start | bytes 393216 | tf_op jit(solution)/shard_map/all_to_all | solution.py:175
  262.2 108.2 %reduce-scatter.2.cloned.1.call-start = ((), (), s32[]{:S(2)}) async-start(), calls=%async_computation.7 | async-start | bytes 2654208 | tf_op jit(solution)/shard_map/reduce_scatter | solution.py:178
  263.7 11.7 %copy-start.3 = (f32[2,384,128]{1,2,0:T(8,128)}, f32[2,384,128]{1,2,0:T(8,128)S(1)}, u32[]{:S(2)}) copy-start(f32[2,384,128]{1,2,0:T(8,128)S(1)} %get-tuple-element.11) | copy-start | bytes 1179652
  263.7 11.7 %copy-start.4 = (f32[2,384,128]{1,2,0:T(8,128)}, f32[2,384,128]{1,2,0:T(8,128)S(1)}, u32[]{:S(2)}) copy-start(f32[2,384,128]{1,2,0:T(8,128)S(1)} %get-tuple-element.12) | copy-start | bytes 1179652
  272.8 2.5 copy-start.8
  275.3 2.1 copy-start.9
  277.5 1.3 copy-start.7
  278.7 0.9 copy-start.14
  279.7 0.9 copy-start.13
  279.7 1.0 copy-start.15
  279.9 1.9 copy-start.5
  281.8 13.1 %slice-start = ((s8[4718592]{0:T(1024)(128)(4,1)}), s8[524288]{0:T(1024)(128)(4,1)S(1)}, s32[]{:S(2)}) async-start(s8[4718592]{0:T(1024)(128)(4,1)} %bitcast.147), calls=%async_computation.8 | async-start | bytes 1048576
  282.8 7.8 %copy-start.22 = (f32[128]{0:T(128)S(1)}, f32[128]{0:T(128)}, u32[]{:S(2)}) copy-start(f32[128]{0:T(128)} %constant.63.clone) | copy-start | bytes 1540
  287.8 4.9 %copy-start.19 = (f32[2,384]{1,0:T(2,128)S(1)}, f32[2,384]{1,0:T(2,128)}, u32[]{:S(2)}) copy-start(f32[2,384]{1,0:T(2,128)} %copy-done.18) | copy-start | bytes 9220
  290.6 4.2 %slice-start.1 = ((s8[4718592]{0:T(1024)(128)(4,1)}), s8[4194304]{0:T(1024)(128)(4,1)S(1)}, s32[]{:S(2)}) async-start(s8[4718592]{0:T(1024)(128)(4,1)} %bitcast.147), calls=%async_computation.9 | async-start | bytes 8388608
  292.7 2.0 copy-start.12
  299.8 19.1 %copy-start.2 = (bf16[1,48,3072]{2,1,0:T(8,128)(2,1)S(1)}, bf16[1,48,3072]{2,1,0:T(8,128)(2,1)}, u32[]{:S(2)}) copy-start(bf16[1,48,3072]{2,1,0:T(8,128)(2,1)} %param.13) | copy-start | bytes 884740
  299.8 19.1 %copy-start.17 = (f32[3072]{0:T(1024)S(1)}, f32[3072]{0:T(1024)}, u32[]{:S(2)}) copy-start(f32[3072]{0:T(1024)} %copy-done.16) | copy-start | bytes 36868
  318.9 51.6 %copy-start.21 = (f32[48]{0:T(128)S(1)}, f32[48]{0:T(128)}, u32[]{:S(2)}) copy-start(f32[48]{0:T(128)} %copy-done.20) | copy-start | bytes 580
  318.9 51.6 %copy-start.24 = (f32[48]{0:T(128)S(1)}, f32[48]{0:T(128)}, u32[]{:S(2)}) copy-start(f32[48]{0:T(128)} %copy-done.23) | copy-start | bytes 580
  318.9 52.8 %copy-start.11 = (bf16[1,48,3072]{2,1,0:T(8,128)(2,1)S(1)}, bf16[1,48,3072]{2,1,0:T(8,128)(2,1)}, u32[]{:S(2)}) copy-start(bf16[1,48,3072]{2,1,0:T(8,128)(2,1)} %param.19) | copy-start | bytes 884740
Sparse Core Ops, SparseCore 0:
  10.2 62.9 all-gather.10
  74.7 36.1 all-gather.8
  113.7 51.8 all-gather.6
  166.9 80.6 all-gather.12
  298.5 71.9 reduce-scatter.1
